TPU v7x, 256 devices: a whole 4x4x8 slice. The times are simulated.
256 devices in a mesh: depth: 4 (over z_lo, core), scan: 64 (over z_hi, x, y).
Axes of the slice: x: 4, y: 4, z: 8 (z_hi: 4, z_lo: 2; z = z_hi * 2 + z_lo), core: 2. Of those that a mesh axis runs over, the one named last changes fastest.
Arguments:
- probe_wave: bfloat16 [2, 512, 512], replicated, may hold values from -6 to 6
- prop_rows: bfloat16 [2, 512, 512], replicated, may hold values from -0.1875 to 0.1875
- prop_cols: bfloat16 [2, 512, 512], replicated, may hold values from -0.1875 to 0.1875
- transmission: bfloat16 [4, 2, 768, 768], P('depth', None, 'scan'), may hold values from -0.5 to 1.3, as said below
- exit_cotangent: bfloat16 [128, 2, 512, 512], P('scan'), may hold values from -1.1953125 to 1.1953125
- window_tiles: int32 [128, 2], P('scan'), may hold values from 0 to 8
- slot_count: int32 [64], P('scan'), may hold values from 1 to 2, as said below
Outputs:
- object_grad: float32 [4, 2, 768, 768], P('depth', None, 'scan')
Inputs may be any that keep to these rules, and one draw needn't show every extreme that they name: `window_tiles`: a window starts 32 times these indices and stays inside the slice. The first slot_count[j] slots of scan index j are used and the others are ignored; some scan index uses all 2 slots and some uses one. `transmission`: real parts lie in 0.6 to 1.3 and imaginary parts in -0.5 to 0.5.
All inputs are finite; a program needn't handle non-finite values.
Results may differ from a plain program's by a relative error of at most 0.014.
Values may be sent and summed in bfloat16 or wider, within the bound.
No kernel may reach another device: no remote copies, remote signals or barrier semaphores. Data moves between devices by JAX's collectives and lax.ppermute only.
A program may use at most 128 MiB of HBM per device.

v0:
```python
import jax
import jax.numpy as jnp
from jax import lax
from jax.sharding import PartitionSpec as P

TILE = 32


def shifted(value, axis, steps):
    count = lax.axis_size(axis)
    leading, last = (max(0, -steps), min(count, count - steps))
    return lax.ppermute(value, axis, [(source, source + steps) for source in range(leading, last)])


def rows_product(matrix, field):
    real = jnp.dot(matrix[0], field[0], preferred_element_type=jnp.float32) - jnp.dot(
        matrix[1], field[1], preferred_element_type=jnp.float32
    )
    imag = jnp.dot(matrix[0], field[1], preferred_element_type=jnp.float32) + jnp.dot(
        matrix[1], field[0], preferred_element_type=jnp.float32
    )
    return jnp.stack([real, imag])


def right_transpose(left, right):
    return lax.dot_general(
        left, right, (((1,), (1,)), ((), ())), preferred_element_type=jnp.float32
    )


def cols_product(field, matrix):
    real = right_transpose(field[0], matrix[0]) - right_transpose(field[1], matrix[1])
    imag = right_transpose(field[1], matrix[0]) + right_transpose(field[0], matrix[1])
    return jnp.stack([real, imag])


def left_transpose(left, right):
    return lax.dot_general(
        left, right, (((0,), (0,)), ((), ())), preferred_element_type=jnp.float32
    )


def adjoint_rows(matrix, field):
    real = left_transpose(matrix[0], field[0]) + left_transpose(matrix[1], field[1])
    imag = left_transpose(matrix[0], field[1]) - left_transpose(matrix[1], field[0])
    return jnp.stack([real, imag])


def conj_cols(field, matrix):
    real = jnp.dot(field[0], matrix[0], preferred_element_type=jnp.float32) + jnp.dot(
        field[1], matrix[1], preferred_element_type=jnp.float32
    )
    imag = jnp.dot(field[1], matrix[0], preferred_element_type=jnp.float32) - jnp.dot(
        field[0], matrix[1], preferred_element_type=jnp.float32
    )
    return jnp.stack([real, imag])


def complex_times(first, second):
    a0 = first[0].astype(jnp.float32)
    a1 = first[1].astype(jnp.float32)
    b0 = second[0].astype(jnp.float32)
    b1 = second[1].astype(jnp.float32)
    return jnp.stack([a0 * b0 - a1 * b1, a0 * b1 + a1 * b0])


def conj_times(first, second):
    a0 = first[0].astype(jnp.float32)
    a1 = first[1].astype(jnp.float32)
    b0 = second[0]
    b1 = second[1]
    return jnp.stack([a0 * b0 + a1 * b1, a0 * b1 - a1 * b0])


def on_device(
    probe_wave, prop_rows, prop_cols, transmission, exit_cotangent, window_tiles, slot_count
):
    depth_count = lax.axis_size("depth")
    depth_index = lax.axis_index("depth")
    slots = exit_cotangent.shape[0]
    width = probe_wave.shape[-1]
    ticks = slots + depth_count - 1
    used_slots = slot_count[0]
    whole = lax.all_gather(transmission[0], "scan", axis=1, tiled=True)
    zero = jnp.zeros((), jnp.int32)

    def window_start(slot):
        return (window_tiles[slot, 0] * TILE, window_tiles[slot, 1] * TILE)

    def patch_of(slot):
        row_start, col_start = window_start(slot)
        return lax.dynamic_slice(whole, (zero, row_start, col_start), (2, width, width))

    empty_wave = jnp.zeros((2, width, width), jnp.bfloat16)
    stored = jnp.zeros((slots, 2, width, width), jnp.bfloat16)
    incoming = empty_wave
    for tick in range(ticks):
        slot = tick - depth_index
        active = (slot >= 0) & (slot < slots) & (slot < used_slots)
        safe = jnp.clip(slot, 0, slots - 1)
        wave = jnp.where(depth_index == 0, probe_wave, incoming)
        kept = jnp.where(active, wave, stored[safe])
        stored = lax.dynamic_update_index_in_dim(stored, kept, safe, 0)

        def advance():
            product = complex_times(wave, patch_of(safe)).astype(jnp.bfloat16)
            swept = rows_product(prop_rows, product).astype(jnp.bfloat16)
            return cols_product(swept, prop_cols).astype(jnp.bfloat16)

        outgoing = lax.cond(active & (depth_index < depth_count - 1), advance, lambda: empty_wave)
        incoming = shifted(outgoing, "depth", 1)
    grad = jnp.zeros(whole.shape, jnp.float32)
    incoming = empty_wave
    empty_term = jnp.zeros((2, width, width), jnp.float32)
    for tick in range(ticks):
        slot = tick - (depth_count - 1 - depth_index)
        active = (slot >= 0) & (slot < slots) & (slot < used_slots)
        safe = jnp.clip(slot, 0, slots - 1)
        upstream = jnp.where(depth_index == depth_count - 1, exit_cotangent[safe], incoming)

        def retreat():
            swept = adjoint_rows(prop_rows, upstream).astype(jnp.bfloat16)
            adjoint = conj_cols(swept, prop_cols)
            contrib = conj_times(stored[safe], adjoint)
            return (contrib, conj_times(patch_of(safe), adjoint).astype(jnp.bfloat16))

        contrib, outgoing = lax.cond(active, retreat, lambda: (empty_term, empty_wave))
        row_start, col_start = window_start(safe)
        current = lax.dynamic_slice(grad, (zero, row_start, col_start), (2, width, width))
        grad = lax.dynamic_update_slice(grad, current + contrib, (zero, row_start, col_start))
        incoming = shifted(outgoing, "depth", -1)
    total = lax.psum_scatter(grad, "scan", scatter_dimension=1, tiled=True)
    return total[None]


def solution(mesh):
    placed = (
        P(),
        P(),
        P(),
        P("depth", None, "scan", None),
        P("scan", None, None, None),
        P("scan", None),
        P("scan"),
    )
    return jax.shard_map(
        on_device,
        mesh=mesh,
        in_specs=placed,
        out_specs=P("depth", None, "scan", None),
        check_vma=False,
    )
```

profile of v0, /device:TPU:8, one launch (start us, length us, event | category | flops | bytes accessed | tf_op | source)
XLA Modules:
  0.0 1586.8 jit_solution(9367382944052077562)
XLA Ops:
  8.0 1.6 broadcast_in_dim.41
  9.5 1.8 bitcast_dynamic-update-slice_fusion.4
  11.3 81.5 %all-gather.3.cloned.1.call-done = bf16[1,2,768,768]{3,1,0,2:T(2,128)(2,1)} async-done(((bf16[1,2,12,768]{3,1,0,2:T(2,128)(2,1)}), bf16[1,2,768,768]{3,1,0,2:T(2,128)(2,1)}) %all-gather.3.cloned.1.call-update) | async-done | bytes 2359312 | tf_op jit(solution)/shard_map/all_gather | solution.py:84
  92.8 12.7 conditional.9
  92.8 3.4 copy.15
  98.0 2.4 fusion.11
  105.5 2.2 collective-permute-start
  107.7 1.3 constant_dynamic-slice_fusion.24
  109.4 1.8 bitcast_dynamic-update-slice_fusion.3
  112.3 16.7 %collective-permute-start.1 = (bf16[2,512,512]{2,1,0:T(8,128)(2,1)}, bf16[2,512,512]{2,1,0:T(8,128)(2,1)}, u32[]{:S(2)}, u32[]{:S(2)}) collective-permute-start(bf16[2,512,512]{2,1,0:T(8,128)(2,1)} %get-tuple-element.591), channel_id=1, source_target_pairs={{0,64},{64,128},{128,192},{1,65},{65,129},{129,193},{2,66},{66,130... | collective-permute-start | bytes 3145736 | tf_op jit(solution)/shard_map/ppermute | solution.py:12
  129.0 1.3 constant_dynamic-slice_fusion.23
  130.3 1.8 bitcast_dynamic-update-slice_fusion.2
  133.2 13.4 collective-permute-start.2
  146.6 1.3 constant_dynamic-slice_fusion.22
  148.2 1.8 bitcast_dynamic-update-slice_fusion.1
  151.1 27.8 %collective-permute-start.3 = (bf16[2,512,512]{2,1,0:T(8,128)(2,1)}, bf16[2,512,512]{2,1,0:T(8,128)(2,1)}, u32[]{:S(2)}, u32[]{:S(2)}) collective-permute-start(bf16[2,512,512]{2,1,0:T(8,128)(2,1)} %get-tuple-element.593), channel_id=1, source_target_pairs={{0,64},{64,128},{128,192},{1,65},{65,129},{129,193},{2,66},{66,130... | collective-permute-start | bytes 3145736 | tf_op jit(solution)/shard_map/ppermute | solution.py:12
  178.9 1.3 constant_dynamic-slice_fusion.21
  180.6 1.5 bitcast_dynamic-update-slice_fusion
  182.0 3.1 conditional.13
  183.3 1.9 broadcast_in_dim.27.clone
  186.4 16.1 %collective-permute-done.4 = bf16[2,512,512]{2,1,0:T(8,128)(2,1)S(1)} collective-permute-done((bf16[2,512,512]{2,1,0:T(8,128)(2,1)}, bf16[2,512,512]{2,1,0:T(8,128)(2,1)S(1)}, u32[]{:S(2)}, u32[]{:S(2)}) %collective-permute-start.4) | collective-permute-done | bytes 1048608 | tf_op jit(solution)/shard_map/ppermute | solution.py:12
  202.5 3.1 conditional.14
  203.6 1.9 broadcast_in_dim.28.clone
  205.6 1.3 collective-permute-start.5
  206.9 15.8 collective-permute-done.5
  222.7 3.2 conditional.15
  223.7 2.0 broadcast_in_dim.29.clone
  227.2 44.8 %collective-permute-done.6 = bf16[2,512,512]{2,1,0:T(8,128)(2,1)S(1)} collective-permute-done((bf16[2,512,512]{2,1,0:T(8,128)(2,1)}, bf16[2,512,512]{2,1,0:T(8,128)(2,1)S(1)}, u32[]{:S(2)}, u32[]{:S(2)}) %collective-permute-start.6) | collective-permute-done | bytes 1048608 | tf_op jit(solution)/shard_map/ppermute | solution.py:12
  272.0 19.2 %conditional.16 = (bf16[2,512,512]{2,1,0:T(8,128)(2,1)}, f32[2,512,512]{2,0,1:T(2,128)}) conditional(s32[]{:T(128)} %convert_element_type.243, () %tuple.81, (s32[]{:T(128)}, bf16[2,2,512,512]{3,2,1,0:T(8,128)(2,1)}, bf16[2,512,512]{2,1,0:T(8,128)(2,1)S(1)}, pred[]{:T(512)}, bf16[2,512,512]{2,1,0:T(8,128)(2,1)S(1)}, ...), branch_computations={%region_14.15_spmd, %region_15.16_spmd.clone.clone} | conditional | flops 2155347968 | bytes 47710424 | solution.py:127
  272.5 1.3 bitcast_select_fusion.2
  276.2 1.4 convolution_subtract_fusion.14
  277.6 3.4 copy.44
  284.2 2.9 fusion.227
  288.3 3.0 copy.45
  291.3 1.5 collective-permute-start.7
  299.8 3.4 broadcast_in_dim.40
  303.2 95.6 %dynamic_update_slice.36 = f32[2,768,768]{2,0,1:T(2,128)} dynamic-update-slice(f32[2,768,768]{2,0,1:T(2,128)} %broadcast_in_dim.40, f32[2,512,512]{2,0,1:T(2,128)} %get-tuple-element.413, s32[]{:T(128)} %constant.173.clone.1, s32[]{:T(128)S(6)} %select_n.250, s32[]{:T(128)S(6)} %select_n.251) | dynamic-update-slice | bytes 4194308 | tf_op jit(solution)/shard_map/dynamic_update_slice | solution.py:130
  398.8 5.9 dynamic-slice_add_fusion.3
  404.7 95.6 %dynamic_update_slice.37 = f32[2,768,768]{2,0,1:T(2,128)} dynamic-update-slice(f32[2,768,768]{2,0,1:T(2,128)} %dynamic_update_slice.36, f32[2,512,512]{2,0,1:T(2,128)} %dynamic-slice_add_fusion.3, s32[]{:T(128)} %constant.173.clone.1, s32[]{:T(128)S(6)} %select_n.252, s32[]{:T(128)S(6)} %select_n.253) | dynamic-update-slice | bytes 4194308 | tf_op jit(solution)/shard_map/dynamic_update_slice | solution.py:130
  500.3 5.9 dynamic-slice_add_fusion.2
  506.2 95.6 %dynamic_update_slice.38 = f32[2,768,768]{2,0,1:T(2,128)} dynamic-update-slice(f32[2,768,768]{2,0,1:T(2,128)} %dynamic_update_slice.37, f32[2,512,512]{2,0,1:T(2,128)} %dynamic-slice_add_fusion.2, s32[]{:T(128)} %constant.173.clone.1, s32[]{:T(128)S(6)} %select_n.256, s32[]{:T(128)S(6)} %select_n.257) | dynamic-update-slice | bytes 4194308 | tf_op jit(solution)/shard_map/dynamic_update_slice | solution.py:130
  601.8 5.9 dynamic-slice_add_fusion.1
  607.7 95.6 %dynamic_update_slice.39 = f32[2,768,768]{2,0,1:T(2,128)} dynamic-update-slice(f32[2,768,768]{2,0,1:T(2,128)} %dynamic_update_slice.38, f32[2,512,512]{2,0,1:T(2,128)} %dynamic-slice_add_fusion.1, s32[]{:T(128)} %constant.173.clone.1, s32[]{:T(128)S(6)} %select_n.259, s32[]{:T(128)S(6)} %select_n.260) | dynamic-update-slice | bytes 4194308 | tf_op jit(solution)/shard_map/dynamic_update_slice | solution.py:130
  704.0 1.3 copy-done.4
  705.4 4.6 dynamic-slice_add_fusion
  710.0 39.7 %dynamic_update_slice.40 = f32[2,768,768]{2,0,1:T(2,128)} dynamic-update-slice(f32[2,768,768]{2,0,1:T(2,128)} %dynamic_update_slice.39, f32[2,512,512]{2,0,1:T(2,128)S(1)} %dynamic-slice_add_fusion, s32[]{:T(128)} %constant.173.clone.1, s32[]{:T(128)S(6)} %select_n.262, s32[]{:T(128)S(6)} %select_n.263) | dynamic-update-slice | bytes 4194308 | tf_op jit(solution)/shard_map/dynamic_update_slice | solution.py:130
  751.6 826.7 %all-reduce.3.cloned.1.call-done = f32[2,768,768]{2,0,1:T(2,128)} async-done(((f32[2,768,768]{2,0,1:T(2,128)}), f32[2,768,768]{2,0,1:T(2,128)}) %all-reduce.3.cloned.1.call-update) | async-done | bytes 4718608
  1578.2 1.5 dynamic-slice_bitcast_fusion.18
  (58 shorter events, 28.1 us)
Async XLA Ops:
  6.5 3.0 copy-start.2
  6.5 86.3 %all-gather.3.cloned.1.call-start = ((), (), s32[]{:S(2)}) async-start(), calls=%async_computation | async-start | bytes 2396160 | tf_op jit(solution)/shard_map/all_gather | solution.py:84
  7.3 1571.0 %all-reduce.3.cloned.1.call-start = ((), (), s32[]{:S(2)}) async-start(), calls=%async_computation.1 | async-start | bytes 9437184
  9.5 83.3 %copy-start = (bf16[2,512,512]{2,1,0:T(8,128)(2,1)S(1)}, bf16[2,512,512]{2,1,0:T(8,128)(2,1)}, u32[]{:S(2)}) copy-start(bf16[2,512,512]{2,1,0:T(8,128)(2,1)} %param.27) | copy-start | bytes 3145732
  9.5 83.3 %copy-start.1 = (bf16[2,512,512]{2,1,0:T(8,128)(2,1)S(1)}, bf16[2,512,512]{2,1,0:T(8,128)(2,1)}, u32[]{:S(2)}) copy-start(bf16[2,512,512]{2,1,0:T(8,128)(2,1)} %param.26) | copy-start | bytes 3145732
  9.5 83.3 %copy-start.9 = (s32[2,2]{1,0:T(2,128)S(1)}, s32[2,2]{1,0:T(2,128)}, u32[]{:S(2)}) copy-start(s32[2,2]{1,0:T(2,128)} %param.30) | copy-start | bytes 52
  105.5 3.9 collective-permute-start
  112.3 18.0 %collective-permute-start.1 = (bf16[2,512,512]{2,1,0:T(8,128)(2,1)}, bf16[2,512,512]{2,1,0:T(8,128)(2,1)}, u32[]{:S(2)}, u32[]{:S(2)}) collective-permute-start(bf16[2,512,512]{2,1,0:T(8,128)(2,1)} %get-tuple-element.591), channel_id=1, source_target_pairs={{0,64},{64,128},{128,192},{1,65},{65,129},{129,193},{2,66},{66,130... | collective-permute-start | bytes 3145736 | tf_op jit(solution)/shard_map/ppermute | solution.py:12
  133.2 15.0 collective-permute-start.2
  151.1 29.5 %collective-permute-start.3 = (bf16[2,512,512]{2,1,0:T(8,128)(2,1)}, bf16[2,512,512]{2,1,0:T(8,128)(2,1)}, u32[]{:S(2)}, u32[]{:S(2)}) collective-permute-start(bf16[2,512,512]{2,1,0:T(8,128)(2,1)} %get-tuple-element.593), channel_id=1, source_target_pairs={{0,64},{64,128},{128,192},{1,65},{65,129},{129,193},{2,66},{66,130... | collective-permute-start | bytes 3145736 | tf_op jit(solution)/shard_map/ppermute | solution.py:12
  180.2 1.8 copy-start.3
  185.1 17.4 %collective-permute-start.4 = (bf16[2,512,512]{2,1,0:T(8,128)(2,1)}, bf16[2,512,512]{2,1,0:T(8,128)(2,1)S(1)}, u32[]{:S(2)}, u32[]{:S(2)}) collective-permute-start(bf16[2,512,512]{2,1,0:T(8,128)(2,1)} %get-tuple-element.200), channel_id=1, source_target_pairs={{64,0},{128,64},{192,128},{65,1},{129,65},{193,129},{66,2},{130,66... | collective-permute-start | bytes 3145736 | tf_op jit(solution)/shard_map/ppermute | solution.py:12
  205.6 17.1 %collective-permute-start.5 = (bf16[2,512,512]{2,1,0:T(8,128)(2,1)}, bf16[2,512,512]{2,1,0:T(8,128)(2,1)S(1)}, u32[]{:S(2)}, u32[]{:S(2)}) collective-permute-start(bf16[2,512,512]{2,1,0:T(8,128)(2,1)} %get-tuple-element.202), channel_id=1, source_target_pairs={{64,0},{128,64},{192,128},{65,1},{129,65},{193,129},{66,2},{130,66... | collective-permute-start | bytes 3145736 | tf_op jit(solution)/shard_map/ppermute | solution.py:12
  225.9 46.1 %collective-permute-start.6 = (bf16[2,512,512]{2,1,0:T(8,128)(2,1)}, bf16[2,512,512]{2,1,0:T(8,128)(2,1)S(1)}, u32[]{:S(2)}, u32[]{:S(2)}) collective-permute-start(bf16[2,512,512]{2,1,0:T(8,128)(2,1)} %get-tuple-element.204), channel_id=1, source_target_pairs={{64,0},{128,64},{192,128},{65,1},{129,65},{193,129},{66,2},{130,66... | collective-permute-start | bytes 3145736 | tf_op jit(solution)/shard_map/ppermute | solution.py:12
  282.9 1.2 copy-start.8
  291.3 412.0 %collective-permute-start.7 = (bf16[2,512,512]{2,1,0:T(8,128)(2,1)}, bf16[2,512,512]{2,1,0:T(8,128)(2,1)S(1)}, u32[]{:S(2)}, u32[]{:S(2)}) collective-permute-start(bf16[2,512,512]{2,1,0:T(8,128)(2,1)} %get-tuple-element.206), channel_id=1, source_target_pairs={{64,0},{128,64},{192,128},{65,1},{129,65},{193,129},{66,2},{130,66... | collective-permute-start | bytes 3145736 | tf_op jit(solution)/shard_map/ppermute | solution.py:12
  704.0 1.3 copy-start.4
  749.7 0.7 copy-start.10
Sparse Core Ops, SparseCore 0:
  10.5 82.2 all-gather.2
  749.8 828.3 all-reduce.2
where the time goes:
time: 1610 us; the launch traced here: 1590 us
  waiting for transfers between devices  986 us (61%)
  local copies, waits for them, and re-layouts  461 us (29%)
  starting transfers between devices  65.5 us (4%)
  other arithmetic  37.2 us (2%)
  between operations  21.5 us (1%)
    unnamed x3, waiting for transfers between devices  827 us
    dynamic_update_slice x5, local copies, waits for them, and re-layouts, on_device(): lax.dynamic_update_slice(grad, current + contrib, (zero, row_start, col_s...  422 us
    all_gather x1, waiting for transfers between devices, on_device(): whole = lax.all_gather(transmission[0], 'scan', axis=1, tiled=True)  81.5 us
    ppermute x8, waiting for transfers between devices, shifted(): lax.ppermute(value, axis, [(source, source + steps) for source in range(l...  77.6 us
    ppermute x8, starting transfers between devices, shifted(): lax.ppermute(value, axis, [(source, source + steps) for source in range(l...  65.5 us
  transfers between devices with their start and end apart: 10, of which 8 were waited for; matrix products, arithmetic and copies ran while one was open for 26% of the time, Pallas kernels for 0%

commit v1 on v0

--- a/solution.py
+++ b/solution.py
@@ -1,9 +1,20 @@
+import functools
 import jax
 import jax.numpy as jnp
 from jax import lax
 from jax.sharding import PartitionSpec as P
 
 TILE = 32
+
+
+def _push_panels(arr, k_dim):
+    z1 = lax.psum(1, "scan")
+    v_next = jnp.stack([arr] * z1, axis=0)
+    upper = lax.all_to_all(v_next, "scan", 0, 0)
+    return jnp.concatenate(upper, k_dim)
+
+
+_feed_edges = functools.partial(_push_panels, k_dim=1)
 
 
 def shifted(value, axis, steps):
@@ -81,7 +92,7 @@
     width = probe_wave.shape[-1]
     ticks = slots + depth_count - 1
     used_slots = slot_count[0]
-    whole = lax.all_gather(transmission[0], "scan", axis=1, tiled=True)
+    whole = _feed_edges(transmission[0])
     zero = jnp.zeros((), jnp.int32)
 
     def window_start(slot):

time: 1610 us -> 1590 us (0.988)
  waiting for transfers between devices: 986 us -> 950 us
    all_gather x1 -> x0, waiting for transfers between devices: 81.5 us -> none  [on_device(): whole = lax.all_gather(transmission[0], 'scan', axis=1, tiled=True)]
    all_to_all x0 -> x1, waiting for transfers between devices: none -> 50.4 us  [_push_panels(): upper = lax.all_to_all(v_next, 'scan', 0, 0)]
    unnamed x3 -> x2, waiting for transfers between devices: 827 us -> 822 us
  transfers between devices with their start and end apart: 10 -> 10, of which waited for: 8 -> 9; matrix products, arithmetic and copies ran while one was open for 26% -> 26% of each run, Pallas kernels for 0% -> 0%
where the time goes in v1:
time: 1590 us; the launch traced here: 1570 us
  waiting for transfers between devices  950 us (60%)
  local copies, waits for them, and re-layouts  463 us (29%)
  starting transfers between devices  80 us (5%)
  other arithmetic  36.2 us (2%)
  between operations  21.3 us (1%)
    unnamed x2, waiting for transfers between devices  822 us
    dynamic_update_slice x5, local copies, waits for them, and re-layouts, on_device(): lax.dynamic_update_slice(grad, current + contrib, (zero, row_start, col_s...  424 us
    ppermute x8, waiting for transfers between devices, shifted(): lax.ppermute(value, axis, [(source, source + steps) for source in range(l...  77.3 us
    ppermute x8, starting transfers between devices, shifted(): lax.ppermute(value, axis, [(source, source + steps) for source in range(l...  65.4 us
    all_to_all x1, waiting for transfers between devices, _push_panels(): upper = lax.all_to_all(v_next, 'scan', 0, 0)  50.4 us
  transfers between devices with their start and end apart: 10, of which 9 were waited for; matrix products, arithmetic and copies ran while one was open for 26% of the time, Pallas kernels for 0%

profile of v1, /device:TPU:8, one launch (start us, length us, event | category | flops | bytes accessed | tf_op | source)
XLA Modules:
  0.0 1567.0 jit_solution(17183708722561211244)
XLA Ops:
  6.5 3.4 stack.214
  9.9 14.6 all-to-all-start
  25.2 1.5 broadcast_in_dim.41
  26.7 3.0 bitcast_dynamic-update-slice_fusion.4
  29.6 50.4 %all-to-all-done = bf16[64,2,12,768]{3,1,2,0:T(2,128)(2,1)S(1)} async-done(((bf16[64,2,12,768]{3,1,2,0:T(2,128)(2,1)}), bf16[64,2,12,768]{3,1,2,0:T(2,128)(2,1)S(1)}, u32[]{:S(2)}, u32[]{:S(2)}) %all-to-all-start) | async-done | bytes 2359328 | tf_op jit(solution)/shard_map/all_to_all | solution.py:13
  80.0 11.2 conditional.9
  80.0 1.7 copy.27
  83.7 2.5 fusion.11
  91.2 2.3 collective-permute-start
  95.1 1.8 bitcast_dynamic-update-slice_fusion.3
  96.9 1.5 conditional.10
  98.4 18.1 %collective-permute-start.1 = (bf16[2,512,512]{2,1,0:T(8,128)(2,1)}, bf16[2,512,512]{2,1,0:T(8,128)(2,1)}, u32[]{:S(2)}, u32[]{:S(2)}) collective-permute-start(bf16[2,512,512]{2,1,0:T(8,128)(2,1)} %get-tuple-element.655), channel_id=1, source_target_pairs={{0,64},{64,128},{128,192},{1,65},{65,129},{129,193},{2,66},{66,130... | collective-permute-start | bytes 3145736 | tf_op jit(solution)/shard_map/ppermute | solution.py:23
  116.5 1.4 constant_dynamic-slice_fusion.23
  118.2 1.8 bitcast_dynamic-update-slice_fusion.2
  121.0 13.5 collective-permute-start.2
  136.2 1.8 bitcast_dynamic-update-slice_fusion.1
  139.2 26.1 %collective-permute-start.3 = (bf16[2,512,512]{2,1,0:T(8,128)(2,1)}, bf16[2,512,512]{2,1,0:T(8,128)(2,1)}, u32[]{:S(2)}, u32[]{:S(2)}) collective-permute-start(bf16[2,512,512]{2,1,0:T(8,128)(2,1)} %get-tuple-element.657), channel_id=1, source_target_pairs={{0,64},{64,128},{128,192},{1,65},{65,129},{129,193},{2,66},{66,130... | collective-permute-start | bytes 3145736 | tf_op jit(solution)/shard_map/ppermute | solution.py:23
  165.4 1.4 constant_dynamic-slice_fusion.21
  167.0 1.4 bitcast_dynamic-update-slice_fusion
  169.1 3.0 conditional.13
  170.1 1.9 broadcast_in_dim.27.clone
  173.3 15.5 collective-permute-done.4
  188.9 3.1 conditional.14
  190.1 1.9 broadcast_in_dim.28.clone
  193.3 15.9 %collective-permute-done.5 = bf16[2,512,512]{2,1,0:T(8,128)(2,1)} collective-permute-done((bf16[2,512,512]{2,1,0:T(8,128)(2,1)}, bf16[2,512,512]{2,1,0:T(8,128)(2,1)}, u32[]{:S(2)}, u32[]{:S(2)}) %collective-permute-start.5) | collective-permute-done | bytes 1048608 | tf_op jit(solution)/shard_map/ppermute | solution.py:23
  209.2 3.2 conditional.15
  210.3 1.9 broadcast_in_dim.29.clone
  213.7 45.0 %collective-permute-done.6 = bf16[2,512,512]{2,1,0:T(8,128)(2,1)} collective-permute-done((bf16[2,512,512]{2,1,0:T(8,128)(2,1)}, bf16[2,512,512]{2,1,0:T(8,128)(2,1)}, u32[]{:S(2)}, u32[]{:S(2)}) %collective-permute-start.6) | collective-permute-done | bytes 1048608 | tf_op jit(solution)/shard_map/ppermute | solution.py:23
  258.7 17.7 %conditional.16 = (bf16[2,512,512]{2,1,0:T(8,128)(2,1)}, f32[2,512,512]{2,0,1:T(2,128)S(1)}) conditional(s32[]{:T(128)} %convert_element_type.243, () %tuple.81, (s32[]{:T(128)}, bf16[2,2,512,512]{3,2,1,0:T(8,128)(2,1)}, bf16[2,512,512]{2,1,0:T(8,128)(2,1)}, pred[]{:T(512)}, bf16[2,512,512]{2,1,0:T(8,128)(2,1)S(1)}, ...), branch_computations={%region_14.15_spmd, %region_15.16_spmd.clone.clone} | conditional | flops 2155347968 | bytes 58196296 | solution.py:138
  259.2 1.7 bitcast_select_fusion.2
  264.2 1.5 convolution_subtract_fusion.14
  265.7 1.7 copy.56
  269.2 1.5 fusion.240
  270.7 2.8 fusion.227
  274.8 1.6 copy.57
  276.4 1.5 collective-permute-start.7
  284.8 3.3 broadcast_in_dim.40
  288.1 95.6 %dynamic_update_slice.36 = f32[2,768,768]{2,0,1:T(2,128)} dynamic-update-slice(f32[2,768,768]{2,0,1:T(2,128)} %broadcast_in_dim.40, f32[2,512,512]{2,0,1:T(2,128)} %get-tuple-element.477, s32[]{:T(128)} %constant.173.clone.1, s32[]{:T(128)S(6)} %select_n.250, s32[]{:T(128)S(6)} %select_n.251) | dynamic-update-slice | bytes 4194308 | tf_op jit(solution)/shard_map/dynamic_update_slice | solution.py:141
  383.7 4.6 dynamic-slice_add_fusion.3
  388.3 96.7 %dynamic_update_slice.37 = f32[2,768,768]{2,0,1:T(2,128)} dynamic-update-slice(f32[2,768,768]{2,0,1:T(2,128)} %dynamic_update_slice.36, f32[2,512,512]{2,0,1:T(2,128)S(1)} %dynamic-slice_add_fusion.3, s32[]{:T(128)} %constant.173.clone.1, s32[]{:T(128)S(6)} %select_n.252, s32[]{:T(128)S(6)} %select_n.253) | dynamic-update-slice | bytes 4194308 | tf_op jit(solution)/shard_map/dynamic_update_slice | solution.py:141
  485.0 4.6 dynamic-slice_add_fusion.2
  489.6 96.7 %dynamic_update_slice.38 = f32[2,768,768]{2,0,1:T(2,128)} dynamic-update-slice(f32[2,768,768]{2,0,1:T(2,128)} %dynamic_update_slice.37, f32[2,512,512]{2,0,1:T(2,128)S(1)} %dynamic-slice_add_fusion.2, s32[]{:T(128)} %constant.173.clone.1, s32[]{:T(128)S(6)} %select_n.256, s32[]{:T(128)S(6)} %select_n.257) | dynamic-update-slice | bytes 4194308 | tf_op jit(solution)/shard_map/dynamic_update_slice | solution.py:141
  586.3 6.0 dynamic-slice_add_fusion.1
  592.2 95.7 %dynamic_update_slice.39 = f32[2,768,768]{2,0,1:T(2,128)} dynamic-update-slice(f32[2,768,768]{2,0,1:T(2,128)} %dynamic_update_slice.38, f32[2,512,512]{2,0,1:T(2,128)} %dynamic-slice_add_fusion.1, s32[]{:T(128)} %constant.173.clone.1, s32[]{:T(128)S(6)} %select_n.259, s32[]{:T(128)S(6)} %select_n.260) | dynamic-update-slice | bytes 4194308 | tf_op jit(solution)/shard_map/dynamic_update_slice | solution.py:141
  690.0 4.6 dynamic-slice_add_fusion
  694.6 39.7 %dynamic_update_slice.40 = f32[2,768,768]{2,0,1:T(2,128)} dynamic-update-slice(f32[2,768,768]{2,0,1:T(2,128)} %dynamic_update_slice.39, f32[2,512,512]{2,0,1:T(2,128)S(1)} %dynamic-slice_add_fusion, s32[]{:T(128)} %constant.173.clone.1, s32[]{:T(128)S(6)} %select_n.262, s32[]{:T(128)S(6)} %select_n.263) | dynamic-update-slice | bytes 4194308 | tf_op jit(solution)/shard_map/dynamic_update_slice | solution.py:141
  736.2 822.1 %all-reduce.3.cloned.1.call-done = f32[2,768,768]{2,0,1:T(2,128)} async-done(((f32[2,768,768]{2,0,1:T(2,128)}), f32[2,768,768]{2,0,1:T(2,128)}) %all-reduce.3.cloned.1.call-update) | async-done | bytes 4718608
  1558.4 1.5 dynamic-slice_bitcast_fusion.18
  (78 shorter events, 32.1 us)
Async XLA Ops:
  9.9 70.1 %all-to-all-start = ((bf16[64,2,12,768]{3,1,2,0:T(2,128)(2,1)}), bf16[64,2,12,768]{3,1,2,0:T(2,128)(2,1)S(1)}, u32[]{:S(2)}, u32[]{:S(2)}) async-start(bf16[64,2,12,768]{3,1,2,0:T(2,128)(2,1)} %stack.214), calls=%async_computation | async-start | bytes 4718592 | tf_op jit(solution)/shard_map/all_to_all | solution.py:13
  24.5 1533.9 %all-reduce.3.cloned.1.call-start = ((), (), s32[]{:S(2)}) async-start(), calls=%async_computation.1 | async-start | bytes 9437184
  26.7 53.4 %copy-start = (bf16[2,512,512]{2,1,0:T(8,128)(2,1)S(1)}, bf16[2,512,512]{2,1,0:T(8,128)(2,1)}, u32[]{:S(2)}) copy-start(bf16[2,512,512]{2,1,0:T(8,128)(2,1)} %param.27) | copy-start | bytes 3145732
  26.7 53.4 %copy-start.33 = (s32[2,2]{1,0:T(2,128)S(1)}, s32[2,2]{1,0:T(2,128)}, u32[]{:S(2)}) copy-start(s32[2,2]{1,0:T(2,128)} %param.30) | copy-start | bytes 52
  83.7 2.5 copy-start.3
  91.2 3.9 collective-permute-start
  93.5 1.6 copy-start.10
  98.4 19.7 %collective-permute-start.1 = (bf16[2,512,512]{2,1,0:T(8,128)(2,1)}, bf16[2,512,512]{2,1,0:T(8,128)(2,1)}, u32[]{:S(2)}, u32[]{:S(2)}) collective-permute-start(bf16[2,512,512]{2,1,0:T(8,128)(2,1)} %get-tuple-element.655), channel_id=1, source_target_pairs={{0,64},{64,128},{128,192},{1,65},{65,129},{129,193},{2,66},{66,130... | collective-permute-start | bytes 3145736 | tf_op jit(solution)/shard_map/ppermute | solution.py:23
  116.5 1.6 copy-start.11
  121.0 15.2 collective-permute-start.2
  134.6 1.6 copy-start.12
  139.2 27.8 %collective-permute-start.3 = (bf16[2,512,512]{2,1,0:T(8,128)(2,1)}, bf16[2,512,512]{2,1,0:T(8,128)(2,1)}, u32[]{:S(2)}, u32[]{:S(2)}) collective-permute-start(bf16[2,512,512]{2,1,0:T(8,128)(2,1)} %get-tuple-element.657), channel_id=1, source_target_pairs={{0,64},{64,128},{128,192},{1,65},{65,129},{129,193},{2,66},{66,130... | collective-permute-start | bytes 3145736 | tf_op jit(solution)/shard_map/ppermute | solution.py:23
  165.4 1.6 copy-start.13
  166.8 1.7 copy-start.1
  166.8 2.3 copy-start.14
  172.0 16.8 %collective-permute-start.4 = (bf16[2,512,512]{2,1,0:T(8,128)(2,1)}, bf16[2,512,512]{2,1,0:T(8,128)(2,1)}, u32[]{:S(2)}, u32[]{:S(2)}) collective-permute-start(bf16[2,512,512]{2,1,0:T(8,128)(2,1)} %get-tuple-element.200), channel_id=1, source_target_pairs={{64,0},{128,64},{192,128},{65,1},{129,65},{193,129},{66,2},{130,66... | collective-permute-start | bytes 3145736 | tf_op jit(solution)/shard_map/ppermute | solution.py:23
  192.0 17.2 %collective-permute-start.5 = (bf16[2,512,512]{2,1,0:T(8,128)(2,1)}, bf16[2,512,512]{2,1,0:T(8,128)(2,1)}, u32[]{:S(2)}, u32[]{:S(2)}) collective-permute-start(bf16[2,512,512]{2,1,0:T(8,128)(2,1)} %get-tuple-element.202), channel_id=1, source_target_pairs={{64,0},{128,64},{192,128},{65,1},{129,65},{193,129},{66,2},{130,66... | collective-permute-start | bytes 3145736 | tf_op jit(solution)/shard_map/ppermute | solution.py:23
  212.4 46.3 %collective-permute-start.6 = (bf16[2,512,512]{2,1,0:T(8,128)(2,1)}, bf16[2,512,512]{2,1,0:T(8,128)(2,1)}, u32[]{:S(2)}, u32[]{:S(2)}) collective-permute-start(bf16[2,512,512]{2,1,0:T(8,128)(2,1)} %get-tuple-element.204), channel_id=1, source_target_pairs={{64,0},{128,64},{192,128},{65,1},{129,65},{193,129},{66,2},{130,66... | collective-permute-start | bytes 3145736 | tf_op jit(solution)/shard_map/ppermute | solution.py:23
  259.2 1.9 copy-start.9
  262.0 0.9 copy-start.23
  263.4 0.8 copy-start.28
  267.4 3.3 copy-start.24
  267.4 3.3 copy-start.32
  276.4 11.7 copy-start.15
  276.4 411.4 %collective-permute-start.7 = (bf16[2,512,512]{2,1,0:T(8,128)(2,1)}, bf16[2,512,512]{2,1,0:T(8,128)(2,1)}, u32[]{:S(2)}, u32[]{:S(2)}) collective-permute-start(bf16[2,512,512]{2,1,0:T(8,128)(2,1)} %get-tuple-element.206), channel_id=1, source_target_pairs={{64,0},{128,64},{192,128},{65,1},{129,65},{193,129},{66,2},{130,66... | collective-permute-start | bytes 3145736 | tf_op jit(solution)/shard_map/ppermute | solution.py:23
  592.2 95.7 %copy-start.2 = (bf16[2,512,512]{2,1,0:T(8,128)(2,1)S(1)}, bf16[2,512,512]{2,1,0:T(8,128)(2,1)}, u32[]{:S(2)}) copy-start(bf16[2,512,512]{2,1,0:T(8,128)(2,1)} %param.26) | copy-start | bytes 3145732
  688.7 1.3 copy-start.16
  734.3 0.7 copy-start.34
Sparse Core Ops, SparseCore 0:
  734.5 823.8 all-reduce.2
